TPU v7x, 256 devices: a whole 4x4x8 slice. The times are simulated.
256 devices in a mesh: shot: 8 (over x, y_lo), domain: 32 (over z, y_hi, core).
Axes of the slice: x: 4, y: 4 (y_hi: 2, y_lo: 2; y = y_hi * 2 + y_lo), z: 8, core: 2. Of those that a mesh axis runs over, the one named last changes fastest.
Arguments:
- velsq: float32 [64, 256, 128], P('domain', 'shot'), may hold values from 0.04 to 0.12
- epsilon: float32 [64, 256, 128], P('domain', 'shot'), may hold values from 0 to 0.3
- delta: float32 [64, 256, 128], P('domain', 'shot'), may hold values from 0 to 0.15
- tilt: float32 [64, 256, 128], P('domain', 'shot'), may hold values from -1.2 to 1.2
- azimuth: float32 [64, 256, 128], P('domain', 'shot'), may hold values from -3.140625 to 3.140625
- forward_state: float32 [8, 4, 64, 256, 128], P('shot', None, 'domain'), may hold values from -6 to 6
- adjoint_state: float32 [8, 4, 64, 256, 128], P('shot', None, 'domain'), may hold values from -6 to 6
- wavelet: float32 [8, 2], P('shot'), may hold values from -60 to 60
- source: int32 [8], P('shot'), may hold values from 0 to 2097151
- receivers: int32 [8, 256], P('shot'), may hold values from 0 to 2097151
- observed: float32 [8, 2, 256], P('shot'), may hold values from -18 to 18
Outputs:
- gradients: float32 [5, 64, 256, 128], P(None, 'domain', 'shot')
Inputs may be any that keep to these rules, and one draw needn't show every extreme that they name: `source`: flat index x * 256 * 128 + y * 128 + z of a grid cell. `receivers`: flat index x * 256 * 128 + y * 128 + z of a grid cell; cells may repeat.
All inputs are finite; a program needn't handle non-finite values.
Results may differ from a plain program's by a relative error of at most 0.0001.
Values sent between devices are 32-bit elements; how exact they have to be, the bound alone decides.
A program may use at most 128 MiB of HBM per device.

v0:
```python
import jax
import jax.numpy as jnp
from jax import lax
from jax.sharding import PartitionSpec as P

STEPS = 2


def with_halo(block, sides, width):
    for axis, dim in sides:
        count = lax.axis_size(axis)
        forward = [(i, i + 1) for i in range(count - 1)]
        backward = [(target, source) for source, target in forward]
        low = lax.ppermute(
            lax.slice_in_dim(block, block.shape[dim] - width, None, axis=dim), axis, forward
        )
        high = lax.ppermute(lax.slice_in_dim(block, 0, width, axis=dim), axis, backward)
        block = jnp.concatenate([low, block, high], axis=dim)
    return block


def hessian(values):
    padded = jnp.pad(values, ((0, 0), (1, 1), (1, 1)))
    center = padded[1:-1, 1:-1, 1:-1]
    curve_xx = padded[2:, 1:-1, 1:-1] + padded[:-2, 1:-1, 1:-1] - 2.0 * center
    curve_yy = padded[1:-1, 2:, 1:-1] + padded[1:-1, :-2, 1:-1] - 2.0 * center
    curve_zz = padded[1:-1, 1:-1, 2:] + padded[1:-1, 1:-1, :-2] - 2.0 * center
    mixed_xy = 0.25 * (
        padded[2:, 2:, 1:-1]
        - padded[2:, :-2, 1:-1]
        - padded[:-2, 2:, 1:-1]
        + padded[:-2, :-2, 1:-1]
    )
    mixed_xz = 0.25 * (
        padded[2:, 1:-1, 2:]
        - padded[2:, 1:-1, :-2]
        - padded[:-2, 1:-1, 2:]
        + padded[:-2, 1:-1, :-2]
    )
    mixed_yz = 0.25 * (
        padded[1:-1, 2:, 2:]
        - padded[1:-1, 2:, :-2]
        - padded[1:-1, :-2, 2:]
        + padded[1:-1, :-2, :-2]
    )
    return jnp.stack([curve_xx, curve_yy, curve_zz, mixed_xy, mixed_xz, mixed_yz])


def tables(velsq, epsilon, delta, tilt, azimuth):
    sin_tilt = jnp.sin(tilt)
    cos_tilt = jnp.cos(tilt)
    sin_azim = jnp.sin(azimuth)
    cos_azim = jnp.cos(azimuth)
    axis_x = sin_tilt * cos_azim
    axis_y = sin_tilt * sin_azim
    turn_x = cos_tilt * cos_azim
    turn_y = cos_tilt * sin_azim
    turn_z = -sin_tilt
    spin_x = -sin_tilt * sin_azim
    spin_y = sin_tilt * cos_azim
    along = jnp.stack(
        [
            axis_x * axis_x,
            axis_y * axis_y,
            cos_tilt * cos_tilt,
            2.0 * axis_x * axis_y,
            2.0 * axis_x * cos_tilt,
            2.0 * axis_y * cos_tilt,
        ]
    )
    by_tilt = jnp.stack(
        [
            2.0 * turn_x * axis_x,
            2.0 * turn_y * axis_y,
            2.0 * turn_z * cos_tilt,
            2.0 * (turn_x * axis_y + turn_y * axis_x),
            2.0 * (turn_x * cos_tilt + turn_z * axis_x),
            2.0 * (turn_y * cos_tilt + turn_z * axis_y),
        ]
    )
    by_spin = jnp.stack(
        [
            2.0 * spin_x * axis_x,
            2.0 * spin_y * axis_y,
            jnp.zeros_like(cos_tilt),
            2.0 * (spin_x * axis_y + spin_y * axis_x),
            2.0 * spin_x * cos_tilt,
            2.0 * spin_y * cos_tilt,
        ]
    )
    return (velsq, 1.0 + 2.0 * epsilon, jnp.sqrt(1.0 + 2.0 * delta), along, by_tilt, by_spin)


def operate(pad_p, pad_q, table, full):
    speed_sq, stretch, root_d, along, by_tilt, by_spin = table
    hess_p = hessian(pad_p)
    hess_q = hessian(pad_q)
    laplace = hess_p[0] + hess_p[1] + hess_p[2]
    axial_p = jnp.sum(along * hess_p, axis=0)
    axial_q = jnp.sum(along * hess_q, axis=0)
    across = laplace - axial_p
    drive_p = stretch * across + root_d * axial_q
    drive_q = root_d * across + axial_q
    if full:
        image_terms = (
            across,
            axial_q,
            jnp.sum(by_tilt * hess_p, axis=0),
            jnp.sum(by_tilt * hess_q, axis=0),
            jnp.sum(by_spin * hess_p, axis=0),
            jnp.sum(by_spin * hess_q, axis=0),
        )
        return (drive_p, drive_q, image_terms)
    return (drive_p, drive_q, ())


def advance(pad_p, pad_q, prior_p, prior_q, table, full):
    drive_p, drive_q, image_terms = operate(pad_p, pad_q, table, full)
    speed_sq = table[0]
    next_p = 2.0 * pad_p[1:-1] - prior_p + speed_sq * drive_p
    next_q = 2.0 * pad_q[1:-1] - prior_q + speed_sq * drive_q
    return (next_p, next_q, image_terms)


def correlate(gradient, adjoint_p, adjoint_q, image_terms, table):
    speed_sq, stretch, root_d, along, by_tilt, by_spin = table
    across, axial_q, tilt_p, tilt_q, spin_p, spin_q = image_terms
    g_speed = (
        gradient[0]
        + adjoint_p * (stretch * across + root_d * axial_q)
        + adjoint_q * (root_d * across + axial_q)
    )
    g_eps = gradient[1] + 2.0 * speed_sq * adjoint_p * across
    g_delta = gradient[2] + speed_sq * (adjoint_p * axial_q + adjoint_q * across) / root_d
    g_tilt = gradient[3] + speed_sq * (
        adjoint_p * (root_d * tilt_q - stretch * tilt_p) + adjoint_q * (tilt_q - root_d * tilt_p)
    )
    g_spin = gradient[4] + speed_sq * (
        adjoint_p * (root_d * spin_q - stretch * spin_p) + adjoint_q * (spin_q - root_d * spin_p)
    )
    return (g_speed, g_eps, g_delta, g_tilt, g_spin)


def inject(values, start_row, target, amount):
    layout = values.shape
    plane_size = layout[1] * layout[2]
    offset = target - start_row * plane_size
    inside = (offset >= 0) & (offset < layout[0] * plane_size)
    clipped = jnp.where(inside, offset, 0)
    return values.reshape(-1).at[clipped].add(jnp.where(inside, amount, 0.0)).reshape(layout)


def sample_cells(values, start_row, target):
    layout = values.shape
    plane_size = layout[1] * layout[2]
    offset = target - start_row * plane_size
    inside = (offset >= 0) & (offset < layout[0] * plane_size)
    clipped = jnp.where(inside, offset, 0)
    return jnp.where(inside, values.reshape(-1)[clipped], 0.0)


def single_rim(field_p, field_q):
    padded = with_halo(jnp.stack([field_p, field_q]), (("domain", 1),), 1)
    return (padded[0], padded[1])


def shards(
    velsq,
    epsilon,
    delta,
    tilt,
    azimuth,
    forward_state,
    adjoint_state,
    wavelet,
    source,
    receivers,
    observed,
):
    gathered = (
        lax.all_gather(velsq, "shot", axis=1, tiled=True),
        lax.all_gather(epsilon, "shot", axis=1, tiled=True),
        lax.all_gather(delta, "shot", axis=1, tiled=True),
        lax.all_gather(tilt, "shot", axis=1, tiled=True),
        lax.all_gather(azimuth, "shot", axis=1, tiled=True),
    )
    row_count = gathered[0].shape[0]
    first_row = lax.axis_index("domain") * row_count
    inner = tables(gathered[0], gathered[1], gathered[2], gathered[3], gathered[4])
    full_terms = False
    full_terms = True
    source_cell = source[0]
    receiver_cells = receivers[0]
    older_p, field_p, older_q, field_q = (
        forward_state[0, 0],
        forward_state[0, 1],
        forward_state[0, 2],
        forward_state[0, 3],
    )
    saved = []
    traces = []
    for moment in range(STEPS):
        pad_p, pad_q = single_rim(field_p, field_q)
        next_p, next_q, image_terms = advance(pad_p, pad_q, older_p, older_q, inner, full_terms)
        next_p = inject(next_p, first_row, source_cell, wavelet[0, moment])
        next_q = inject(next_q, first_row, source_cell, wavelet[0, moment])
        saved.append(image_terms)
        traces.append(sample_cells(next_p, first_row, receiver_cells))
        older_p, field_p, older_q, field_q = (field_p, next_p, field_q, next_q)
    recorded = lax.psum(jnp.stack(traces), "domain")
    misfit = recorded - observed[0]
    gradient = tuple((jnp.zeros(field_p.shape, jnp.float32) for member in range(5)))
    before_p, adjoint_p, before_q, adjoint_q = (
        adjoint_state[0, 0],
        adjoint_state[0, 1],
        adjoint_state[0, 2],
        adjoint_state[0, 3],
    )
    for moment in range(STEPS):
        back_index = STEPS - 1 - moment
        gradient = correlate(gradient, adjoint_p, adjoint_q, saved[back_index], inner)
        pad_p, pad_q = single_rim(adjoint_p, adjoint_q)
        next_p, next_q, unused = advance(pad_p, pad_q, before_p, before_q, inner, False)
        next_p = inject(next_p, first_row, receiver_cells, misfit[back_index])
        before_p, adjoint_p, before_q, adjoint_q = (adjoint_p, next_p, adjoint_q, next_q)
    return lax.psum_scatter(jnp.stack(gradient), "shot", scatter_dimension=2, tiled=True)


def solution(mesh):
    placed = (
        P("domain", "shot", None),
        P("domain", "shot", None),
        P("domain", "shot", None),
        P("domain", "shot", None),
        P("domain", "shot", None),
        P("shot", None, "domain", None, None),
        P("shot", None, "domain", None, None),
        P("shot", None),
        P("shot"),
        P("shot", None),
        P("shot", None, None),
    )
    return jax.shard_map(
        shards,
        mesh=mesh,
        in_specs=placed,
        out_specs=P(None, "domain", "shot", None),
        check_vma=False,
    )
```

profile of v0, /device:TPU:16, one launch (start us, length us, event | category | flops | bytes accessed | tf_op | source)
XLA Modules:
  0.0 354.3 jit_solution(16403042310096619500)
XLA Ops:
  6.5 1.2 slice_bitcast_fusion.9
  8.5 1.9 collective-permute-start.4
  10.4 2.4 collective-permute-start.5
  13.7 4.8 %collective-permute-start = (f32[2,1,256,128]{3,2,1,0:T(8,128)}, f32[2,1,256,128]{3,2,1,0:T(8,128)}, u32[]{:S(2)}, u32[]{:S(2)}) collective-permute-start(f32[2,1,256,128]{3,2,1,0:T(8,128)} %get-tuple-element.99), channel_id=1, source_target_pairs={{1,0},{2,1},{3,2},{4,3},{5,4},{6,5},{7,6},{8,7},{9,8},{10,9},{11,1... | collective-permute-start | bytes 786440 | tf_op jit(solution)/shard_map/ppermute | solution.py:17
  18.5 2.6 collective-permute-start.1
  21.2 28.5 %all_gather.17 = f32[2,256,128]{2,1,0:T(8,128)S(1)} all-gather(f32[2,32,128]{2,1,0:T(8,128)S(1)} %copy-done.35), channel_id=1, replica_groups=mesh['shot'=8,'domain'=32] {'shot'}, dimensions={1}, use_global_device_ids=true | all-gather | bytes 294912 | tf_op jit(solution)/shard_map/all_gather | solution.py:184
  50.6 28.6 %all_gather.18 = f32[2,256,128]{2,1,0:T(8,128)S(1)} all-gather(f32[2,32,128]{2,1,0:T(8,128)S(1)} %copy-done.36), channel_id=1, replica_groups=mesh['shot'=8,'domain'=32] {'shot'}, dimensions={1}, use_global_device_ids=true | all-gather | bytes 294912 | tf_op jit(solution)/shard_map/all_gather | solution.py:185
  80.2 28.4 %all_gather.16 = f32[2,256,128]{2,1,0:T(8,128)S(1)} all-gather(f32[2,32,128]{2,1,0:T(8,128)S(1)} %copy-done.37), channel_id=1, replica_groups=mesh['shot'=8,'domain'=32] {'shot'}, dimensions={1}, use_global_device_ids=true | all-gather | bytes 294912 | tf_op jit(solution)/shard_map/all_gather | solution.py:181
  108.6 28.4 %all_gather.19 = f32[2,256,128]{2,1,0:T(8,128)S(1)} all-gather(f32[2,32,128]{2,1,0:T(8,128)S(1)} %copy-done.38), channel_id=1, replica_groups=mesh['shot'=8,'domain'=32] {'shot'}, dimensions={1}, use_global_device_ids=true | all-gather | bytes 294912 | tf_op jit(solution)/shard_map/all_gather | solution.py:183
  137.0 28.4 %all_gather.15 = f32[2,256,128]{2,1,0:T(8,128)S(1)} all-gather(f32[2,32,128]{2,1,0:T(8,128)S(1)} %copy-done.39), channel_id=1, replica_groups=mesh['shot'=8,'domain'=32] {'shot'}, dimensions={1}, use_global_device_ids=true | all-gather | bytes 294912 | tf_op jit(solution)/shard_map/all_gather | solution.py:182
  175.1 1.1 pad_maximum_fusion.2
  176.3 1.1 copy-done
  177.5 1.9 subtract_dynamic-update-slice_fusion
  182.0 1.5 pad_maximum_fusion
  183.6 1.1 fusion.155
  184.9 1.1 fusion.28
  188.0 2.4 multiply_reduce_fusion.13
  190.4 1.4 fusion.177
  194.7 1.9 collective-permute-start.2
  196.6 2.6 collective-permute-start.3
  200.0 1.7 gather_fusion
  203.9 4.4 %collective-permute-done.3 = f32[2,1,256,128]{3,2,1,0:T(8,128)} collective-permute-done((f32[2,1,256,128]{3,2,1,0:T(8,128)}, f32[2,1,256,128]{3,2,1,0:T(8,128)}, u32[]{:S(2)}, u32[]{:S(2)}) %collective-permute-start.3) | collective-permute-done | bytes 262176 | tf_op jit(solution)/shard_map/ppermute | solution.py:14
  208.3 1.1 pad_maximum_fusion.1
  209.5 1.2 fusion.152
  213.8 5.6 %multiply_reduce_fusion.2 = (f32[2,256,128]{2,1,0:T(8,128)}, f32[2,256,128]{2,1,0:T(8,128)}, f32[2,256,128]{2,1,0:T(8,128)}, f32[2,256,128]{2,1,0:T(8,128)}, f32...) fusion(f32[6,2,256,128]{3,2,1,0:T(8,128)} %bitcast_dynamic-upda, ...), kind=kLoop, calls=%fused_computation.101 | loop fusion | flops 8650752 | bytes 17301504 | tf_op jit(solution)/shard_map/reduce_sum | solution.py:110
  219.4 2.2 fusion.182
  221.8 1.7 gather_fusion.1
  223.5 64.4 %psum.7 = f32[2,256]{1,0:T(2,128)S(1)} all-reduce(f32[2,256]{1,0:T(2,128)S(1)} %pad_maximum_fusion.18), channel_id=1, replica_groups=mesh['shot'=8,'domain'=32] {'domain'}, use_global_device_ids=true, to_apply=%region_6.7 | all-reduce | flops 512 | bytes 4096 | tf_op jit(solution)/shard_map/psum | solution.py:210
  287.9 2.1 fusion.160
  290.0 2.4 scatter_fusion
  292.5 2.0 bitcast_dynamic-update-slice_fusion.13
  298.8 48.7 %reduce-scatter.2.cloned.1.call-done = f32[5,2,32,128]{3,2,1,0:T(8,128)} async-done(((f32[5,2,256,128]{3,2,1,0:T(8,128)}), f32[5,2,32,128]{3,2,1,0:T(8,128)}) %reduce-scatter.2.cloned.1.call-update) | async-done | bytes 163856 | tf_op jit(solution)/shard_map/reduce_scatter | solution.py:226
  (150 shorter events, 29.7 us)
Async XLA Ops:
  6.5 6.3 %copy-start.1 = (f32[1,4,2,256,128]{4,3,2,1,0:T(8,128)S(1)}, f32[1,4,2,256,128]{4,3,2,1,0:T(8,128)}, u32[]{:S(2)}) copy-start(f32[1,4,2,256,128]{4,3,2,1,0:T(8,128)} %param.22) | copy-start | bytes 3145732
  6.5 340.9 %reduce-scatter.2.cloned.1.call-start = ((), (), s32[]{:S(2)}) async-start(), calls=%async_computation.1 | async-start | bytes 1474560 | tf_op jit(solution)/shard_map/reduce_scatter | solution.py:226
  7.7 167.3 %copy-start.11 = (f32[1,2,256,128]{3,2,1,0:T(8,128)}, f32[1,2,256,128]{3,2,1,0:T(8,128)S(1)}, u32[]{:S(2)}) copy-start(f32[1,2,256,128]{3,2,1,0:T(8,128)S(1)} %get-tuple-element.73) | copy-start | bytes 786436
  7.7 167.3 %copy-start.14 = (f32[1,2,256,128]{3,2,1,0:T(8,128)}, f32[1,2,256,128]{3,2,1,0:T(8,128)S(1)}, u32[]{:S(2)}) copy-start(f32[1,2,256,128]{3,2,1,0:T(8,128)S(1)} %get-tuple-element.74) | copy-start | bytes 786436
  7.7 13.5 %copy-start.35 = (f32[2,32,128]{2,1,0:T(8,128)S(1)}, f32[2,32,128]{2,1,0:T(8,128)}, u32[]{:S(2)}) copy-start(f32[2,32,128]{2,1,0:T(8,128)} %param.20) | copy-start | bytes 98308
  8.5 166.6 %collective-permute-start.4 = (f32[2,1,256,128]{3,2,1,0:T(8,128)}, f32[2,1,256,128]{3,2,1,0:T(8,128)}, u32[]{:S(2)}, u32[]{:S(2)}) collective-permute-start(f32[2,1,256,128]{3,2,1,0:T(8,128)} %get-tuple-element.91), channel_id=1, source_target_pairs={{1,0},{2,1},{3,2},{4,3},{5,4},{6,5},{7,6},{8,7},{9,8},{10,9},{11,1... | collective-permute-start | bytes 786440 | tf_op jit(solution)/shard_map/ppermute | solution.py:17
  10.4 40.3 %copy-start.36 = (f32[2,32,128]{2,1,0:T(8,128)S(1)}, f32[2,32,128]{2,1,0:T(8,128)}, u32[]{:S(2)}) copy-start(f32[2,32,128]{2,1,0:T(8,128)} %param.21) | copy-start | bytes 98308
  10.4 164.7 %collective-permute-start.5 = (f32[2,1,256,128]{3,2,1,0:T(8,128)S(1)}, f32[2,1,256,128]{3,2,1,0:T(8,128)}, u32[]{:S(2)}, u32[]{:S(2)}) collective-permute-start(f32[2,1,256,128]{3,2,1,0:T(8,128)S(1)} %get-tuple-element.92), channel_id=1, source_target_pairs={{0,1},{1,2},{2,3},{3,4},{4,5},{5,6},{6,7},{7,8},{8,9},{9,10},{10,1... | collective-permute-start | bytes 786440 | tf_op jit(solution)/shard_map/ppermute | solution.py:14
  12.9 67.3 %copy-start.5 = (f32[1,2,256,128]{3,2,1,0:T(8,128)}, f32[1,2,256,128]{3,2,1,0:T(8,128)S(1)}, u32[]{:S(2)}) copy-start(f32[1,2,256,128]{3,2,1,0:T(8,128)S(1)} %get-tuple-element.86) | copy-start | bytes 786436
  12.9 171.9 %copy-start.3 = (f32[1,2,256,128]{3,2,1,0:T(8,128)}, f32[1,2,256,128]{3,2,1,0:T(8,128)S(1)}, u32[]{:S(2)}) copy-start(f32[1,2,256,128]{3,2,1,0:T(8,128)S(1)} %get-tuple-element.85) | copy-start | bytes 786436
  12.9 67.3 %copy-start.37 = (f32[2,32,128]{2,1,0:T(8,128)S(1)}, f32[2,32,128]{2,1,0:T(8,128)}, u32[]{:S(2)}) copy-start(f32[2,32,128]{2,1,0:T(8,128)} %param.17) | copy-start | bytes 98308
  12.9 95.7 %copy-start.38 = (f32[2,32,128]{2,1,0:T(8,128)S(1)}, f32[2,32,128]{2,1,0:T(8,128)}, u32[]{:S(2)}) copy-start(f32[2,32,128]{2,1,0:T(8,128)} %param.19) | copy-start | bytes 98308
  13.7 123.3 %copy-start.39 = (f32[2,32,128]{2,1,0:T(8,128)S(1)}, f32[2,32,128]{2,1,0:T(8,128)}, u32[]{:S(2)}) copy-start(f32[2,32,128]{2,1,0:T(8,128)} %param.18) | copy-start | bytes 98308
  13.7 151.6 %copy-start.41 = (f32[1,2]{1,0:T(1,128)S(1)}, f32[1,2]{1,0:T(1,128)}, u32[]{:S(2)}) copy-start(f32[1,2]{1,0:T(1,128)} %param.24) | copy-start | bytes 28
  13.7 168.3 %collective-permute-start = (f32[2,1,256,128]{3,2,1,0:T(8,128)}, f32[2,1,256,128]{3,2,1,0:T(8,128)}, u32[]{:S(2)}, u32[]{:S(2)}) collective-permute-start(f32[2,1,256,128]{3,2,1,0:T(8,128)} %get-tuple-element.99), channel_id=1, source_target_pairs={{1,0},{2,1},{3,2},{4,3},{5,4},{6,5},{7,6},{8,7},{9,8},{10,9},{11,1... | collective-permute-start | bytes 786440 | tf_op jit(solution)/shard_map/ppermute | solution.py:17
  18.5 163.5 %collective-permute-start.1 = (f32[2,1,256,128]{3,2,1,0:T(8,128)}, f32[2,1,256,128]{3,2,1,0:T(8,128)}, u32[]{:S(2)}, u32[]{:S(2)}) collective-permute-start(f32[2,1,256,128]{3,2,1,0:T(8,128)} %get-tuple-element.100), channel_id=1, source_target_pairs={{0,1},{1,2},{2,3},{3,4},{4,5},{5,6},{6,7},{7,8},{8,9},{9,10},{10,1... | collective-permute-start | bytes 786440 | tf_op jit(solution)/shard_map/ppermute | solution.py:14
  169.5 1.8 copy-start.40
  180.4 1.6 copy-start.6
  187.3 3.1 copy-start.9
  188.0 2.4 copy-start.7
  188.0 2.4 copy-start.4
  191.8 2.1 copy-start.18
  194.7 9.2 %collective-permute-start.2 = (f32[2,1,256,128]{3,2,1,0:T(8,128)}, f32[2,1,256,128]{3,2,1,0:T(8,128)}, u32[]{:S(2)}, u32[]{:S(2)}) collective-permute-start(f32[2,1,256,128]{3,2,1,0:T(8,128)} %get-tuple-element.97), channel_id=1, source_target_pairs={{1,0},{2,1},{3,2},{4,3},{5,4},{6,5},{7,6},{8,7},{9,8},{10,9},{11,1... | collective-permute-start | bytes 786440 | tf_op jit(solution)/shard_map/ppermute | solution.py:17
  196.6 11.7 %collective-permute-start.3 = (f32[2,1,256,128]{3,2,1,0:T(8,128)}, f32[2,1,256,128]{3,2,1,0:T(8,128)}, u32[]{:S(2)}, u32[]{:S(2)}) collective-permute-start(f32[2,1,256,128]{3,2,1,0:T(8,128)} %get-tuple-element.98), channel_id=1, source_target_pairs={{0,1},{1,2},{2,3},{3,4},{4,5},{5,6},{6,7},{7,8},{8,9},{9,10},{10,1... | collective-permute-start | bytes 786440 | tf_op jit(solution)/shard_map/ppermute | solution.py:14
  211.8 2.0 copy-start.10
  219.4 2.2 copy-start.20
  219.4 68.5 %copy-start.42 = (f32[1,2,256]{2,1,0:T(2,128)S(1)}, f32[1,2,256]{2,1,0:T(2,128)}, u32[]{:S(2)}) copy-start(f32[1,2,256]{2,1,0:T(2,128)} %param.27) | copy-start | bytes 6148
  219.4 68.5 %copy-start.13 = (f32[1,2,256,128]{3,2,1,0:T(8,128)S(1)}, f32[1,2,256,128]{3,2,1,0:T(8,128)}, u32[]{:S(2)}) copy-start(f32[1,2,256,128]{3,2,1,0:T(8,128)} %copy-done.11) | copy-start | bytes 786436
  290.0 2.4 copy-start.17
  290.0 2.4 copy-start.19
  290.0 2.4 copy-start.21
  290.0 2.4 copy-start.23
  (18 other events, 22.3 us)
Sparse Core Ops, SparseCore 0:
  298.9 48.4 reduce-scatter.1
where the time goes:
time: 355 us; the launch traced here: 354 us
  blocking collectives  207 us (58%)
  waiting for transfers between devices  53.1 us (15%)
  other arithmetic  51.8 us (15%)
  starting transfers between devices  16.2 us (5%)
  between operations  16 us (5%)
  local copies, waits for them, and re-layouts  10.5 us (3%)
    psum x1, blocking collectives, shards(): recorded = lax.psum(jnp.stack(traces), 'domain')  64.4 us
    reduce_scatter x1, waiting for transfers between devices, shards(): lax.psum_scatter(jnp.stack(gradient), 'shot', scatter_dimension=2, tiled=...  48.7 us
    all_gather x1, blocking collectives, shards(): lax.all_gather(azimuth, 'shot', axis=1, tiled=True)  28.6 us
    all_gather x1, blocking collectives, shards(): lax.all_gather(tilt, 'shot', axis=1, tiled=True)  28.5 us
    all_gather x1, blocking collectives, shards(): lax.all_gather(velsq, 'shot', axis=1, tiled=True)  28.4 us
    all_gather x1, blocking collectives, shards(): lax.all_gather(delta, 'shot', axis=1, tiled=True)  28.4 us
    all_gather x1, blocking collectives, shards(): lax.all_gather(epsilon, 'shot', axis=1, tiled=True)  28.4 us
    unnamed x33, other arithmetic  22 us
  transfers between devices with their start and end apart: 7, of which 2 were waited for; matrix products, arithmetic and copies ran while one was open for 6% of the time, Pallas kernels for 0%

commit v1 on v0

--- a/solution.py
+++ b/solution.py
@@ -179,7 +179,9 @@
 ):
     gathered = (
         lax.all_gather(velsq, "shot", axis=1, tiled=True),
-        lax.all_gather(epsilon, "shot", axis=1, tiled=True),
+        jnp.concatenate(
+            lax.all_to_all(jnp.stack([epsilon] * lax.axis_size("shot")), "shot", 0, 0), axis=1
+        ),
         lax.all_gather(delta, "shot", axis=1, tiled=True),
         lax.all_gather(tilt, "shot", axis=1, tiled=True),
         lax.all_gather(azimuth, "shot", axis=1, tiled=True),

time: 355 us -> 334 us (0.941)
  blocking collectives: 207 us -> 177 us
  local copies, waits for them, and re-layouts: 10.5 us -> 16.6 us
  starting transfers between devices: 16.2 us -> 21.4 us
  other arithmetic: 51.8 us -> 47 us
    all_gather x1 -> x0, blocking collectives: 28.4 us -> none  [shards(): lax.all_gather(epsilon, 'shot', axis=1, tiled=True)]
    unnamed x86 -> x90, local copies, waits for them, and re-layouts: 3.19 us -> 8.56 us
    all_to_all x0 -> x1, starting transfers between devices: none -> 5.02 us  [shards(): lax.all_to_all(jnp.stack([epsilon] * lax.axis_size('shot')), 'shot', 0, 0)]
    unnamed x33 -> x32, other arithmetic: 22 us -> 17.8 us
  transfers between devices with their start and end apart: 7 -> 8, of which waited for: 2 -> 2; matrix products, arithmetic and copies ran while one was open for 6% -> 6% of each run, Pallas kernels for 0% -> 0%
where the time goes in v1:
time: 334 us; the launch traced here: 333 us
  blocking collectives  177 us (53%)
  waiting for transfers between devices  55.2 us (17%)
  other arithmetic  47 us (14%)
  starting transfers between devices  21.4 us (6%)
  local copies, waits for them, and re-layouts  16.6 us (5%)
  between operations  16 us (5%)
    psum x1, blocking collectives, shards(): recorded = lax.psum(jnp.stack(traces), 'domain')  62.9 us
    reduce_scatter x1, waiting for transfers between devices, shards(): lax.psum_scatter(jnp.stack(gradient), 'shot', scatter_dimension=2, tiled=...  50.4 us
    all_gather x1, blocking collectives, shards(): lax.all_gather(tilt, 'shot', axis=1, tiled=True)  29 us
    all_gather x1, blocking collectives, shards(): lax.all_gather(azimuth, 'shot', axis=1, tiled=True)  28.5 us
    all_gather x1, blocking collectives, shards(): lax.all_gather(delta, 'shot', axis=1, tiled=True)  28.4 us
    all_gather x1, blocking collectives, shards(): lax.all_gather(velsq, 'shot', axis=1, tiled=True)  28.4 us
    unnamed x32, other arithmetic  17.8 us
    ppermute x3, starting transfers between devices, with_halo(): lax.ppermute(lax.slice_in_dim(block, 0, width, axis=dim), axis, backward)  8.73 us
  transfers between devices with their start and end apart: 8, of which 2 were waited for; matrix products, arithmetic and copies ran while one was open for 6% of the time, Pallas kernels for 0%

profile of v1, /device:TPU:16, one launch (start us, length us, event | category | flops | bytes accessed | tf_op | source)
XLA Modules:
  0.0 333.5 jit_solution(17520840737026751404)
XLA Ops:
  6.5 1.2 slice_bitcast_fusion.9
  8.6 2.0 collective-permute-start.4
  10.6 2.4 collective-permute-start.5
  13.9 4.8 %collective-permute-start = (f32[2,1,256,128]{3,2,1,0:T(8,128)}, f32[2,1,256,128]{3,2,1,0:T(8,128)}, u32[]{:S(2)}, u32[]{:S(2)}) collective-permute-start(f32[2,1,256,128]{3,2,1,0:T(8,128)} %get-tuple-element.108), channel_id=1, source_target_pairs={{1,0},{2,1},{3,2},{4,3},{5,4},{6,5},{7,6},{8,7},{9,8},{10,9},{11,1... | collective-permute-start | bytes 786440 | tf_op jit(solution)/shard_map/ppermute | solution.py:17
  18.7 2.6 collective-permute-start.1
  22.1 5.0 %all-to-all-start = ((f32[8,2,32,128]{3,2,1,0:T(8,128)}), f32[8,2,32,128]{3,2,1,0:T(8,128)}, u32[]{:S(2)}, u32[]{:S(2)}) async-start(f32[8,2,32,128]{3,2,1,0:T(8,128)} %stack.213), calls=%async_computation | async-start | bytes 524288 | tf_op jit(solution)/shard_map/all_to_all | solution.py:183
  27.2 29.0 %all_gather.13 = f32[2,256,128]{2,1,0:T(8,128)S(1)} all-gather(f32[2,32,128]{2,1,0:T(8,128)S(1)} %copy-done.38), channel_id=1, replica_groups=mesh['shot'=8,'domain'=32] {'shot'}, dimensions={1}, use_global_device_ids=true | all-gather | bytes 294912 | tf_op jit(solution)/shard_map/all_gather | solution.py:186
  57.2 28.5 %all_gather.14 = f32[2,256,128]{2,1,0:T(8,128)S(1)} all-gather(f32[2,32,128]{2,1,0:T(8,128)S(1)} %copy-done.39), channel_id=1, replica_groups=mesh['shot'=8,'domain'=32] {'shot'}, dimensions={1}, use_global_device_ids=true | all-gather | bytes 294912 | tf_op jit(solution)/shard_map/all_gather | solution.py:187
  86.7 28.4 %all_gather.12 = f32[2,256,128]{2,1,0:T(8,128)S(1)} all-gather(f32[2,32,128]{2,1,0:T(8,128)S(1)} %copy-done.40), channel_id=1, replica_groups=mesh['shot'=8,'domain'=32] {'shot'}, dimensions={1}, use_global_device_ids=true | all-gather | bytes 294912 | tf_op jit(solution)/shard_map/all_gather | solution.py:181
  119.2 1.2 copy-done.3
  120.4 1.1 copy-done.28
  122.9 28.4 %all_gather.15 = f32[2,256,128]{2,1,0:T(8,128)S(1)} all-gather(f32[2,32,128]{2,1,0:T(8,128)S(1)} %copy-done.41), channel_id=1, replica_groups=mesh['shot'=8,'domain'=32] {'shot'}, dimensions={1}, use_global_device_ids=true | all-gather | bytes 294912 | tf_op jit(solution)/shard_map/all_gather | solution.py:185
  160.6 1.2 fusion.140
  161.8 1.1 pad_maximum_fusion
  163.0 1.1 copy-done.2
  164.1 1.2 subtract_dynamic-update-slice_fusion.2
  168.6 2.0 fusion.195
  172.8 1.9 collective-permute-start.2
  174.7 2.6 collective-permute-start.3
  178.3 1.7 gather_fusion
  181.1 1.1 fusion.120
  182.2 4.8 %collective-permute-done.3 = f32[2,1,256,128]{3,2,1,0:T(8,128)} collective-permute-done((f32[2,1,256,128]{3,2,1,0:T(8,128)}, f32[2,1,256,128]{3,2,1,0:T(8,128)}, u32[]{:S(2)}, u32[]{:S(2)}) %collective-permute-start.3) | collective-permute-done | bytes 262176 | tf_op jit(solution)/shard_map/ppermute | solution.py:14
  186.9 1.1 pad_maximum_fusion.1
  188.1 1.2 subtract_dynamic-update-slice_fusion.1
  192.8 5.1 %multiply_reduce_fusion.3 = (f32[2,256,128]{2,1,0:T(8,128)}, f32[2,256,128]{2,1,0:T(8,128)}, f32[2,256,128]{2,1,0:T(8,128)}, f32[2,256,128]{2,1,0:T(8,128)}, f32...) fusion(f32[6,2,256,128]{3,2,1,0:T(8,128)} %bitcast_dynamic-upda, ...), kind=kLoop, calls=%fused_computation.102 | loop fusion | flops 8650752 | bytes 17301504 | tf_op jit(solution)/shard_map/reduce_sum | solution.py:111
  197.9 2.3 fusion.196
  200.3 1.7 gather_fusion.1
  202.1 62.9 %psum.7 = f32[2,256]{1,0:T(2,128)S(1)} all-reduce(f32[2,256]{1,0:T(2,128)S(1)} %pad_maximum_fusion.18), channel_id=1, replica_groups=mesh['shot'=8,'domain'=32] {'domain'}, use_global_device_ids=true, to_apply=%region_6.7 | all-reduce | flops 512 | bytes 4096 | tf_op jit(solution)/shard_map/psum | solution.py:212
  265.0 2.5 fusion.160
  267.5 2.4 scatter_fusion
  270.0 1.5 fusion.194
  276.2 50.4 %reduce-scatter.2.cloned.1.call-done = f32[5,2,32,128]{3,2,1,0:T(8,128)} async-done(((f32[5,2,256,128]{3,2,1,0:T(8,128)}), f32[5,2,32,128]{3,2,1,0:T(8,128)}) %reduce-scatter.2.cloned.1.call-update) | async-done | bytes 163856 | tf_op jit(solution)/shard_map/reduce_scatter | solution.py:228
  (157 shorter events, 33.1 us)
Async XLA Ops:
  6.5 6.5 %copy-start.1 = (f32[1,4,2,256,128]{4,3,2,1,0:T(8,128)S(1)}, f32[1,4,2,256,128]{4,3,2,1,0:T(8,128)}, u32[]{:S(2)}) copy-start(f32[1,4,2,256,128]{4,3,2,1,0:T(8,128)} %param.22) | copy-start | bytes 3145732
  7.7 148.1 %copy-start.12 = (f32[1,2,256,128]{3,2,1,0:T(8,128)}, f32[1,2,256,128]{3,2,1,0:T(8,128)S(1)}, u32[]{:S(2)}) copy-start(f32[1,2,256,128]{3,2,1,0:T(8,128)S(1)} %get-tuple-element.79) | copy-start | bytes 786436
  7.7 148.1 %copy-start.13 = (f32[1,2,256,128]{3,2,1,0:T(8,128)}, f32[1,2,256,128]{3,2,1,0:T(8,128)S(1)}, u32[]{:S(2)}) copy-start(f32[1,2,256,128]{3,2,1,0:T(8,128)S(1)} %get-tuple-element.80) | copy-start | bytes 786436
  7.7 13.7 %copy-start.37 = (f32[2,32,128]{2,1,0:T(8,128)S(1)}, f32[2,32,128]{2,1,0:T(8,128)}, u32[]{:S(2)}) copy-start(f32[2,32,128]{2,1,0:T(8,128)} %param.18) | copy-start | bytes 98308
  8.6 18.6 %copy-start.38 = (f32[2,32,128]{2,1,0:T(8,128)S(1)}, f32[2,32,128]{2,1,0:T(8,128)}, u32[]{:S(2)}) copy-start(f32[2,32,128]{2,1,0:T(8,128)} %param.20) | copy-start | bytes 98308
  8.6 145.6 %collective-permute-start.4 = (f32[2,1,256,128]{3,2,1,0:T(8,128)}, f32[2,1,256,128]{3,2,1,0:T(8,128)S(1)}, u32[]{:S(2)}, u32[]{:S(2)}) collective-permute-start(f32[2,1,256,128]{3,2,1,0:T(8,128)} %get-tuple-element.99), channel_id=1, source_target_pairs={{1,0},{2,1},{3,2},{4,3},{5,4},{6,5},{7,6},{8,7},{9,8},{10,9},{11,1... | collective-permute-start | bytes 786440 | tf_op jit(solution)/shard_map/ppermute | solution.py:17
  10.6 143.6 %collective-permute-start.5 = (f32[2,1,256,128]{3,2,1,0:T(8,128)}, f32[2,1,256,128]{3,2,1,0:T(8,128)S(1)}, u32[]{:S(2)}, u32[]{:S(2)}) collective-permute-start(f32[2,1,256,128]{3,2,1,0:T(8,128)} %get-tuple-element.100), channel_id=1, source_target_pairs={{0,1},{1,2},{2,3},{3,4},{4,5},{5,6},{6,7},{7,8},{8,9},{9,10},{10,1... | collective-permute-start | bytes 786440 | tf_op jit(solution)/shard_map/ppermute | solution.py:14
  13.1 44.1 %copy-start.39 = (f32[2,32,128]{2,1,0:T(8,128)S(1)}, f32[2,32,128]{2,1,0:T(8,128)}, u32[]{:S(2)}) copy-start(f32[2,32,128]{2,1,0:T(8,128)} %param.21) | copy-start | bytes 98308
  13.9 72.8 %copy-start.40 = (f32[2,32,128]{2,1,0:T(8,128)S(1)}, f32[2,32,128]{2,1,0:T(8,128)}, u32[]{:S(2)}) copy-start(f32[2,32,128]{2,1,0:T(8,128)} %param.17) | copy-start | bytes 98308
  13.9 147.9 %collective-permute-start = (f32[2,1,256,128]{3,2,1,0:T(8,128)}, f32[2,1,256,128]{3,2,1,0:T(8,128)}, u32[]{:S(2)}, u32[]{:S(2)}) collective-permute-start(f32[2,1,256,128]{3,2,1,0:T(8,128)} %get-tuple-element.108), channel_id=1, source_target_pairs={{1,0},{2,1},{3,2},{4,3},{5,4},{6,5},{7,6},{8,7},{9,8},{10,9},{11,1... | collective-permute-start | bytes 786440 | tf_op jit(solution)/shard_map/ppermute | solution.py:17
  18.7 143.1 %collective-permute-start.1 = (f32[2,1,256,128]{3,2,1,0:T(8,128)}, f32[2,1,256,128]{3,2,1,0:T(8,128)}, u32[]{:S(2)}, u32[]{:S(2)}) collective-permute-start(f32[2,1,256,128]{3,2,1,0:T(8,128)} %get-tuple-element.109), channel_id=1, source_target_pairs={{0,1},{1,2},{2,3},{3,4},{4,5},{5,6},{6,7},{7,8},{8,9},{9,10},{10,1... | collective-permute-start | bytes 786440 | tf_op jit(solution)/shard_map/ppermute | solution.py:14
  22.1 131.1 %all-to-all-start = ((f32[8,2,32,128]{3,2,1,0:T(8,128)}), f32[8,2,32,128]{3,2,1,0:T(8,128)}, u32[]{:S(2)}, u32[]{:S(2)}) async-start(f32[8,2,32,128]{3,2,1,0:T(8,128)} %stack.213), calls=%async_computation | async-start | bytes 524288 | tf_op jit(solution)/shard_map/all_to_all | solution.py:183
  27.1 299.5 %reduce-scatter.2.cloned.1.call-start = ((), (), s32[]{:S(2)}) async-start(), calls=%async_computation.2 | async-start | bytes 1474560 | tf_op jit(solution)/shard_map/reduce_scatter | solution.py:228
  118.4 3.9 %copy-start.42 = (s32[1,256]{1,0:T(1,128)S(1)}, s32[1,256]{1,0:T(1,128)}, u32[]{:S(2)}) copy-start(s32[1,256]{1,0:T(1,128)} %param.26) | copy-start | bytes 3076
  118.4 3.9 %copy-start.43 = (f32[1,2]{1,0:T(1,128)S(1)}, f32[1,2]{1,0:T(1,128)}, u32[]{:S(2)}) copy-start(f32[1,2]{1,0:T(1,128)} %param.24) | copy-start | bytes 28
  118.4 4.5 %copy-start.41 = (f32[2,32,128]{2,1,0:T(8,128)S(1)}, f32[2,32,128]{2,1,0:T(8,128)}, u32[]{:S(2)}) copy-start(f32[2,32,128]{2,1,0:T(8,128)} %param.19) | copy-start | bytes 98308
  160.6 2.4 copy-start.30
  170.6 2.2 copy-start.10
  171.2 18.2 %copy-start.16 = (f32[65536]{0:T(1024)}, f32[65536]{0:T(1024)S(1)}, u32[]{:S(2)}) copy-start(f32[65536]{0:T(1024)S(1)} %broadcast_multiply_fusion.1) | copy-start | bytes 786436
  172.8 9.4 %collective-permute-start.2 = (f32[2,1,256,128]{3,2,1,0:T(8,128)}, f32[2,1,256,128]{3,2,1,0:T(8,128)}, u32[]{:S(2)}, u32[]{:S(2)}) collective-permute-start(f32[2,1,256,128]{3,2,1,0:T(8,128)} %get-tuple-element.105), channel_id=1, source_target_pairs={{1,0},{2,1},{3,2},{4,3},{5,4},{6,5},{7,6},{8,7},{9,8},{10,9},{11,1... | collective-permute-start | bytes 786440 | tf_op jit(solution)/shard_map/ppermute | solution.py:17
  174.7 12.3 %collective-permute-start.3 = (f32[2,1,256,128]{3,2,1,0:T(8,128)}, f32[2,1,256,128]{3,2,1,0:T(8,128)}, u32[]{:S(2)}, u32[]{:S(2)}) collective-permute-start(f32[2,1,256,128]{3,2,1,0:T(8,128)} %get-tuple-element.106), channel_id=1, source_target_pairs={{0,1},{1,2},{2,3},{3,4},{4,5},{5,6},{6,7},{7,8},{8,9},{9,10},{10,1... | collective-permute-start | bytes 786440 | tf_op jit(solution)/shard_map/ppermute | solution.py:14
  189.3 2.2 copy-start.31
  189.6 1.9 copy-start.29
  190.1 1.8 copy-start.9
  190.5 1.9 copy-start.5
  190.5 2.3 copy-start.7
  192.8 5.1 %copy-start.17 = (f32[65536]{0:T(1024)S(1)}, f32[65536]{0:T(1024)}, u32[]{:S(2)}) copy-start(f32[65536]{0:T(1024)} %copy-done.16) | copy-start | bytes 786436
  197.9 2.3 copy-start.14
  197.9 67.1 %copy-start.44 = (f32[1,2,256]{2,1,0:T(2,128)S(1)}, f32[1,2,256]{2,1,0:T(2,128)}, u32[]{:S(2)}) copy-start(f32[1,2,256]{2,1,0:T(2,128)} %param.27) | copy-start | bytes 6148
  267.5 2.4 copy-start.19
  267.5 2.4 copy-start.20
  269.9 1.6 copy-start.11
  (21 other events, 25.0 us)
Sparse Core Ops, SparseCore 0:
  276.4 50.2 reduce-scatter.1
